TPU v7x, 32 devices: a whole 2x2x4 slice. The times are simulated.
32 devices in a mesh: dp: 8 (over z, y), ctx: 4 (over x, core).
Axes of the slice: x: 2, y: 2, z: 4, core: 2. Of those that a mesh axis runs over, the one named last changes fastest.
Arguments:
- tokens: bfloat16 [8, 512, 2048], P('dp', 'ctx'), may hold values from -6 to 6
- segment_ids: int32 [8, 512], P('dp', 'ctx'), may hold values from 0 to 2, as said below
- positions: int32 [8, 512], P('dp', 'ctx'), may hold values from 0 to 511, as said below
- attn_gain: bfloat16 [2048], P(('dp', 'ctx')), may hold values from 0.5 to 1.5
- w_query: bfloat16 [2048, 2048], P(('dp', 'ctx')), may hold values from -0.125 to 0.125
- w_key: bfloat16 [2048, 512], P(('dp', 'ctx')), may hold values from -0.125 to 0.125
- w_value: bfloat16 [2048, 512], P(('dp', 'ctx')), may hold values from -0.125 to 0.125
- w_output: bfloat16 [2048, 2048], P(('dp', 'ctx')), may hold values from -1 to 1
- ffn_gain: bfloat16 [2048], P(('dp', 'ctx')), may hold values from 0.5 to 1.5
- w_gate: bfloat16 [2048, 8192], P('dp', 'ctx'), may hold values from -0.125 to 0.125
- w_up: bfloat16 [2048, 8192], P('dp', 'ctx'), may hold values from -0.125 to 0.125
- w_down: bfloat16 [8192, 2048], P('ctx', 'dp'), may hold values from -0.125 to 0.125
- cotangent: bfloat16 [8, 512, 2048], P('dp', 'ctx'), may hold values from -6 to 6
Outputs:
- mixed: bfloat16 [8, 512, 2048], P('dp', 'ctx')
- grad_tokens: float32 [8, 512, 2048], P('dp', 'ctx')
- grad_attn_gain: float32 [2048], P(('dp', 'ctx'))
- grad_query: float32 [2048, 2048], P(('dp', 'ctx'))
- grad_key: float32 [2048, 512], P(('dp', 'ctx'))
- grad_value: float32 [2048, 512], P(('dp', 'ctx'))
- grad_output: float32 [2048, 2048], P(('dp', 'ctx'))
- grad_ffn_gain: float32 [2048], P(('dp', 'ctx'))
- grad_gate: float32 [2048, 8192], P('dp', 'ctx')
- grad_up: float32 [2048, 8192], P('dp', 'ctx')
- grad_down: float32 [8192, 2048], P('ctx', 'dp')
Inputs may be any that keep to these rules, and one draw needn't show every extreme that they name: `segment_ids`: along each packed sequence of 512 tokens the document number never falls and starts at 0; documents do not cross sequences. `positions`: 0 at a document's first token and rising by one along the document; the first packed sequence holds a single document.
All inputs are finite; a program needn't handle non-finite values.
Results may differ from a plain program's by a relative error of at most 0.018.
Values may be sent and summed in bfloat16 or wider, within the bound.
No kernel may reach another device: no remote copies, remote signals or barrier semaphores. Data moves between devices by JAX's collectives and lax.ppermute only.
A program may use at most 256 MiB of HBM per device.

v0:
```python
import jax
import jax.numpy as jnp
from jax import lax
from jax.sharding import PartitionSpec as P

QUERY_HEADS = 32
KEY_VALUE_HEADS = 8
HEAD_WIDTH = 64
EPS_NORM = 1e-05
ROPE_BASE = 500000.0
MASKED = -1e30


def rope_tables(where_pos, half_width):
    freqs = ROPE_BASE ** (-(jnp.arange(half_width, dtype=jnp.float32) / half_width))
    angles = where_pos.astype(jnp.float32)[..., None] * freqs
    return (jnp.cos(angles), jnp.sin(angles))


def apply_rotation(values, cosine_table, sine_table):
    half_width = values.shape[-1] // 2
    first = values[..., :half_width]
    second = values[..., half_width:]
    cosine_table = cosine_table[..., None, :]
    sine_table = sine_table[..., None, :]
    return jnp.concatenate(
        [first * cosine_table - second * sine_table, second * cosine_table + first * sine_table],
        axis=-1,
    )


def reverse_rotation(grads, cosine_table, sine_table):
    half_width = grads.shape[-1] // 2
    first = grads[..., :half_width]
    second = grads[..., half_width:]
    cosine_table = cosine_table[..., None, :]
    sine_table = sine_table[..., None, :]
    return jnp.concatenate(
        [first * cosine_table + second * sine_table, second * cosine_table - first * sine_table],
        axis=-1,
    )


def norm_back(upstream, normed, inverse, gain):
    scaled = upstream * gain
    return inverse * (scaled - normed * jnp.mean(scaled * normed, axis=-1, keepdims=True))


def tdot(left, right):
    return lax.dot_general(
        left, right, (((0,), (0,)), ((), ())), preferred_element_type=jnp.float32
    )


def body(
    tokens,
    segment_ids,
    positions,
    attn_gain,
    w_query,
    w_key,
    w_value,
    w_output,
    ffn_gain,
    w_gate,
    w_up,
    w_down,
    cotangent,
):
    local_sequence, context_rows, width = tokens.shape
    token_rows = local_sequence * context_rows
    count_ctx = lax.axis_size("ctx")
    sequence_length = context_rows * count_ctx
    group_rows = local_sequence * sequence_length
    query_groups = QUERY_HEADS // KEY_VALUE_HEADS
    factor = 1.0 / HEAD_WIDTH**0.5
    gain_one, gain_two, wquery, key_weight, value_weight, output_weight = (
        lax.all_gather(attn_gain, ("dp", "ctx"), axis=0, tiled=True),
        lax.all_gather(ffn_gain, ("dp", "ctx"), axis=0, tiled=True),
        lax.all_gather(w_query, ("dp", "ctx"), axis=0, tiled=True),
        lax.all_gather(w_key, ("dp", "ctx"), axis=0, tiled=True),
        lax.all_gather(w_value, ("dp", "ctx"), axis=0, tiled=True),
        lax.all_gather(w_output, ("dp", "ctx"), axis=0, tiled=True),
    )
    gain_onef = gain_one.astype(jnp.float32)
    gain_twof = gain_two.astype(jnp.float32)
    xfloat = tokens.reshape(token_rows, width).astype(jnp.float32)
    inv_one = lax.rsqrt(jnp.mean(xfloat * xfloat, axis=-1, keepdims=True) + EPS_NORM)
    normed_one = xfloat * inv_one
    hidden_first = (normed_one * gain_onef).astype(jnp.bfloat16)
    query_rows = jnp.dot(hidden_first, wquery, preferred_element_type=jnp.float32).reshape(
        local_sequence, context_rows, QUERY_HEADS, HEAD_WIDTH
    )
    unrotated_key = jnp.dot(hidden_first, key_weight, preferred_element_type=jnp.float32).reshape(
        local_sequence, context_rows, KEY_VALUE_HEADS, HEAD_WIDTH
    )
    value_own = (
        jnp.dot(hidden_first, value_weight, preferred_element_type=jnp.float32)
        .astype(jnp.bfloat16)
        .reshape(local_sequence, context_rows, KEY_VALUE_HEADS * HEAD_WIDTH)
    )
    cosine_table, sine_table = rope_tables(positions, HEAD_WIDTH // 2)
    rotated_query = (
        apply_rotation(query_rows, cosine_table, sine_table)
        .astype(jnp.bfloat16)
        .reshape(local_sequence, context_rows, KEY_VALUE_HEADS, query_groups, HEAD_WIDTH)
    )
    rkey_own = (
        apply_rotation(unrotated_key, cosine_table, sine_table)
        .astype(jnp.bfloat16)
        .reshape(local_sequence, context_rows, KEY_VALUE_HEADS * HEAD_WIDTH)
    )
    gathered_keys, gathered_values = (
        lax.all_gather(rkey_own, "ctx", axis=1, tiled=True),
        lax.all_gather(value_own, "ctx", axis=1, tiled=True),
    )
    segments_all = lax.all_gather(segment_ids, "ctx", axis=1, tiled=True)
    gathered_keys = gathered_keys.reshape(
        local_sequence, sequence_length, KEY_VALUE_HEADS, HEAD_WIDTH
    )
    gathered_values = gathered_values.reshape(
        local_sequence, sequence_length, KEY_VALUE_HEADS, HEAD_WIDTH
    )
    query_index = lax.axis_index("ctx") * context_rows + jnp.arange(context_rows, dtype=jnp.int32)
    key_index = jnp.arange(sequence_length, dtype=jnp.int32)
    allowed = (segment_ids[:, :, None] == segments_all[:, None, :]) & (
        key_index[None, None, :] <= query_index[None, :, None]
    )
    allowed = allowed[:, None, None]
    scores = (
        jnp.einsum(
            "schgd,slhd->shgcl", rotated_query, gathered_keys, preferred_element_type=jnp.float32
        )
        * factor
    )
    masked = jnp.where(allowed, scores, MASKED)
    expo = jnp.exp(masked)
    total = jnp.sum(expo, axis=-1, keepdims=True)
    lse = jnp.log(total)
    probs = (expo / total).astype(jnp.bfloat16)
    attended = jnp.einsum(
        "shgcl,slhd->schgd", probs, gathered_values, preferred_element_type=jnp.float32
    )
    attended = attended.astype(jnp.bfloat16).reshape(token_rows, QUERY_HEADS * HEAD_WIDTH)
    resid = xfloat + jnp.dot(attended, output_weight, preferred_element_type=jnp.float32)
    wgate, wup_proj, wdown = (
        lax.all_gather(w_gate, "dp", axis=0, tiled=True),
        lax.all_gather(w_up, "dp", axis=0, tiled=True),
        lax.all_gather(w_down, "dp", axis=1, tiled=True),
    )
    inv_two = lax.rsqrt(jnp.mean(resid * resid, axis=-1, keepdims=True) + EPS_NORM)
    normed_two = resid * inv_two
    h_two = (normed_two * gain_twof).astype(jnp.bfloat16)
    h_group, cot_group = (
        lax.all_gather(
            h_two.reshape(local_sequence, context_rows, width), "ctx", axis=1, tiled=True
        ),
        lax.all_gather(cotangent, "ctx", axis=1, tiled=True),
    )
    h_group = h_group.reshape(group_rows, width)
    cot_group = cot_group.reshape(group_rows, width)
    gate = jnp.dot(h_group, wgate, preferred_element_type=jnp.float32)
    up_proj = jnp.dot(h_group, wup_proj, preferred_element_type=jnp.float32)
    sigma = jax.nn.sigmoid(gate)
    hidden = (gate * sigma * up_proj).astype(jnp.bfloat16)
    partial_out = jnp.dot(hidden, wdown, preferred_element_type=jnp.float32).reshape(
        local_sequence, sequence_length, width
    )
    ffn_out = (
        lax.psum_scatter(partial_out.astype(jnp.bfloat16), "ctx", scatter_dimension=1, tiled=True)
        .astype(jnp.float32)
        .reshape(token_rows, width)
    )
    mixed = (resid + ffn_out).astype(jnp.bfloat16)
    cot_rows = cotangent.reshape(token_rows, width)
    d_hidden = jnp.dot(cot_group, wdown.T, preferred_element_type=jnp.float32)
    d_up = (d_hidden * gate * sigma).astype(jnp.bfloat16)
    d_gate = (d_hidden * up_proj * sigma * (1.0 + gate * (1.0 - sigma))).astype(jnp.bfloat16)
    ffn_sums = lax.psum_scatter(
        jnp.concatenate(
            [tdot(h_group, d_gate), tdot(h_group, d_up), tdot(cot_group, hidden)], axis=1
        ).astype(jnp.bfloat16),
        "dp",
        scatter_dimension=0,
        tiled=True,
    ).astype(jnp.float32)
    ff_width = w_gate.shape[1]
    grad_gate = ffn_sums[:, :ff_width]
    grad_up = ffn_sums[:, ff_width : 2 * ff_width]
    grad_down = ffn_sums[:, 2 * ff_width :].T
    d_h_part = jnp.dot(d_gate, wgate.T, preferred_element_type=jnp.float32) + jnp.dot(
        d_up, wup_proj.T, preferred_element_type=jnp.float32
    )
    d_h_two = (
        lax.psum_scatter(
            d_h_part.reshape(local_sequence, sequence_length, width).astype(jnp.bfloat16),
            "ctx",
            scatter_dimension=1,
            tiled=True,
        )
        .astype(jnp.float32)
        .reshape(token_rows, width)
    )
    gain_term_two = jnp.sum(d_h_two * normed_two, axis=0)
    d_resid = cot_rows.astype(jnp.float32) + norm_back(d_h_two, normed_two, inv_two, gain_twof)
    residual_gradient_second = d_resid.astype(jnp.bfloat16)
    out_term = tdot(attended, residual_gradient_second)
    attended_gradient = jnp.dot(
        residual_gradient_second, output_weight.T, preferred_element_type=jnp.float32
    ).astype(jnp.bfloat16)
    attended_gradient = attended_gradient.reshape(
        local_sequence, context_rows, KEY_VALUE_HEADS, query_groups, HEAD_WIDTH
    )
    probs_f = jnp.where(allowed, jnp.exp(masked - lse), 0.0)
    d_probs = jnp.einsum(
        "schgd,slhd->shgcl", attended_gradient, gathered_values, preferred_element_type=jnp.float32
    )
    delta = jnp.sum(probs_f * d_probs, axis=-1, keepdims=True)
    d_scores_b = (probs_f * (d_probs - delta) * factor).astype(jnp.bfloat16)
    value_gradient_local = jnp.einsum(
        "shgcl,schgd->slhd",
        probs_f.astype(jnp.bfloat16),
        attended_gradient,
        preferred_element_type=jnp.float32,
    )
    d_rquery = jnp.einsum(
        "shgcl,slhd->schgd", d_scores_b, gathered_keys, preferred_element_type=jnp.float32
    )
    rotated_key_gradient = jnp.einsum(
        "shgcl,schgd->slhd", d_scores_b, rotated_query, preferred_element_type=jnp.float32
    )
    key_gradient, value_gradient = (
        lax.psum_scatter(
            rotated_key_gradient.reshape(
                local_sequence, sequence_length, KEY_VALUE_HEADS * HEAD_WIDTH
            ).astype(jnp.bfloat16),
            "ctx",
            scatter_dimension=1,
            tiled=True,
        ).astype(jnp.float32),
        lax.psum_scatter(
            value_gradient_local.reshape(
                local_sequence, sequence_length, KEY_VALUE_HEADS * HEAD_WIDTH
            ).astype(jnp.bfloat16),
            "ctx",
            scatter_dimension=1,
            tiled=True,
        ).astype(jnp.float32),
    )
    dquery = (
        reverse_rotation(
            d_rquery.reshape(local_sequence, context_rows, QUERY_HEADS, HEAD_WIDTH),
            cosine_table,
            sine_table,
        )
        .astype(jnp.bfloat16)
        .reshape(token_rows, QUERY_HEADS * HEAD_WIDTH)
    )
    dkey = (
        reverse_rotation(
            key_gradient.reshape(local_sequence, context_rows, KEY_VALUE_HEADS, HEAD_WIDTH),
            cosine_table,
            sine_table,
        )
        .astype(jnp.bfloat16)
        .reshape(token_rows, KEY_VALUE_HEADS * HEAD_WIDTH)
    )
    value_gradient_full = value_gradient.astype(jnp.bfloat16).reshape(
        token_rows, KEY_VALUE_HEADS * HEAD_WIDTH
    )
    query_term = tdot(hidden_first, dquery)
    key_term = tdot(hidden_first, dkey)
    value_term = tdot(hidden_first, value_gradient_full)
    d_h_one = jnp.dot(dquery, wquery.T, preferred_element_type=jnp.float32)
    d_h_one = d_h_one + jnp.dot(dkey, key_weight.T, preferred_element_type=jnp.float32)
    d_h_one = d_h_one + jnp.dot(
        value_gradient_full, value_weight.T, preferred_element_type=jnp.float32
    )
    gain_term_one = jnp.sum(d_h_one * normed_one, axis=0)
    grad_tokens = d_resid + norm_back(d_h_one, normed_one, inv_one, gain_onef)
    summed = (
        lax.psum_scatter(gain_term_one, ("dp", "ctx"), scatter_dimension=0, tiled=True),
        lax.psum_scatter(gain_term_two, ("dp", "ctx"), scatter_dimension=0, tiled=True),
        lax.psum_scatter(query_term, ("dp", "ctx"), scatter_dimension=0, tiled=True),
        lax.psum_scatter(key_term, ("dp", "ctx"), scatter_dimension=0, tiled=True),
        lax.psum_scatter(value_term, ("dp", "ctx"), scatter_dimension=0, tiled=True),
        lax.psum_scatter(out_term, ("dp", "ctx"), scatter_dimension=0, tiled=True),
    )
    return (
        mixed.reshape(local_sequence, context_rows, width),
        grad_tokens.reshape(local_sequence, context_rows, width),
        summed[0],
        summed[2],
        summed[3],
        summed[4],
        summed[5],
        summed[1],
        grad_gate,
        grad_up,
        grad_down,
    )


def solution(mesh):
    return jax.shard_map(
        body,
        mesh=mesh,
        in_specs=(
            P("dp", "ctx", None),
            P("dp", "ctx"),
            P("dp", "ctx"),
            P(("dp", "ctx")),
            P(("dp", "ctx"), None),
            P(("dp", "ctx"), None),
            P(("dp", "ctx"), None),
            P(("dp", "ctx"), None),
            P(("dp", "ctx")),
            P("dp", "ctx"),
            P("dp", "ctx"),
            P("ctx", "dp"),
            P("dp", "ctx", None),
        ),
        out_specs=(
            P("dp", "ctx", None),
            P("dp", "ctx", None),
            P(("dp", "ctx")),
            P(("dp", "ctx"), None),
            P(("dp", "ctx"), None),
            P(("dp", "ctx"), None),
            P(("dp", "ctx"), None),
            P(("dp", "ctx")),
            P("dp", "ctx"),
            P("dp", "ctx"),
            P("ctx", "dp"),
        ),
        check_vma=False,
    )
```

profile of v0, /device:TPU:13, one launch (start us, length us, event | category | flops | bytes accessed | tf_op | source)
XLA Modules:
  0.0 1944.1 jit_solution(15713700508738842312)
XLA Ops:
  12.3 39.7 %all-reduce.5 = (bf16[2048]{0:T(1024)(128)(2,1)S(1)}, bf16[2048]{0:T(1024)(128)(2,1)S(1)}) all-reduce(bf16[2048]{0:T(1024)(128)(2,1)S(1)} %dynamic-update-slice, bf16[2048]{0:T(1024)(128)(2,1)S(1)} %dynamic-update-slice.1), channel_id=1, replica_groups=mesh['dp'=8,'ctx'=4] {'dp','ctx'}, use_global_device_ids=true, to_apply=%add | all-reduce | flops 4096 | bytes 16384
  52.1 7.6 all_gather.47
  70.1 7.3 all-gather
  78.4 47.4 %all-gather.14.cloned.1.call-done = bf16[2048,512]{1,0:T(8,128)(2,1)} async-done(((bf16[64,512]{1,0:T(8,128)(2,1)}), bf16[2048,512]{1,0:T(8,128)(2,1)}) %all-gather.14.cloned.1.call-update) | async-done | bytes 2097168 | tf_op jit(solution)/shard_map/all_gather | solution.py:81
  129.6 7.3 all_gather.50
  136.9 68.7 %all-gather.16.cloned.1.call-done = bf16[2048,2048]{1,0:T(8,128)(2,1)} async-done(((bf16[64,2048]{1,0:T(8,128)(2,1)}), bf16[2048,2048]{1,0:T(8,128)(2,1)}) %all-gather.16.cloned.1.call-update) | async-done | bytes 8388624 | tf_op jit(solution)/shard_map/all_gather | solution.py:80
  205.6 12.3 copy.48
  231.4 52.5 %all-gather.18.cloned.1.call-done = bf16[2048,2048]{1,0:T(8,128)(2,1)} async-done(((bf16[64,2048]{1,0:T(8,128)(2,1)}), bf16[2048,2048]{1,0:T(8,128)(2,1)}) %all-gather.18.cloned.1.call-update) | async-done | bytes 8388624 | tf_op jit(solution)/shard_map/all_gather | solution.py:83
  292.3 113.1 %all-gather.20.cloned.1.call-done = bf16[2048,2048]{1,0:T(8,128)(2,1)} async-done(((bf16[256,2048]{1,0:T(8,128)(2,1)}), bf16[2048,2048]{1,0:T(8,128)(2,1)}) %all-gather.20.cloned.1.call-update) | async-done | bytes 8388624 | tf_op jit(solution)/shard_map/all_gather | solution.py:147
  405.3 26.4 %all-gather.28.cloned.1.call-done = bf16[512,2048]{1,0:T(8,128)(2,1)} async-done(((bf16[128,2048]{1,0:T(8,128)(2,1)}), bf16[512,2048]{1,0:T(8,128)(2,1)}) %all-gather.28.cloned.1.call-update) | async-done | bytes 2097168 | tf_op jit(solution)/shard_map/all_gather | solution.py:155
  431.8 10.5 fusion.80
  442.3 112.5 %all-gather.22.cloned.1.call-done = bf16[2048,2048]{1,0:T(8,128)(2,1)} async-done(((bf16[256,2048]{1,0:T(8,128)(2,1)}), bf16[2048,2048]{1,0:T(8,128)(2,1)}) %all-gather.22.cloned.1.call-update) | async-done | bytes 8388624 | tf_op jit(solution)/shard_map/all_gather | solution.py:148
  554.7 10.5 fusion.81
  565.2 15.5 all-gather.26.cloned.1.call-done
  580.8 123.3 %all-gather.24.cloned.1.call-done = bf16[2048,2048]{1,0:T(8,128)(2,1)} async-done(((bf16[2048,256]{1,0:T(8,128)(2,1)}), bf16[2048,2048]{1,0:T(8,128)(2,1)}) %all-gather.24.cloned.1.call-update) | async-done | bytes 8388624 | tf_op jit(solution)/shard_map/all_gather | solution.py:149
  704.1 12.1 multiply_convert_fusion
  716.2 8.0 fusion.82
  724.2 7.4 fusion.11
  731.7 9.9 fusion.10
  741.6 9.6 reduce-scatter.28.cloned.1.call-start
  751.2 10.1 convolution_convert_fusion
  770.2 27.9 %reduce-scatter.14.cloned.1.call-done = bf16[1,128,2048]{2,1,0:T(8,128)(2,1)} async-done(((bf16[1,512,2048]{2,1,0:T(8,128)(2,1)}), bf16[1,128,2048]{2,1,0:T(8,128)(2,1)}) %reduce-scatter.14.cloned.1.call-update) | async-done | bytes 524304 | tf_op jit(solution)/shard_map/reduce_scatter | solution.py:170
  824.9 10.0 convolution_convert_fusion.1
  844.5 19.0 pad_maximum_fusion
  878.8 9.1 fusion.52
  888.0 8.1 fusion.61
  905.2 41.9 %all-reduce.4 = (f32[2048]{0:T(1024)S(1)}, f32[2048]{0:T(1024)S(1)}) all-reduce(f32[2048]{0:T(1024)S(1)} %get-tuple-element.46, f32[2048]{0:T(1024)S(1)} %get-tuple-element.44), channel_id=8, replica_groups=mesh['dp'=8,'ctx'=4] {'dp','ctx'}, use_global_device_ids=true, to_apply=%region_11.12.clone | all-reduce | flops 4096 | bytes 32768
  949.6 328.6 %reduce-scatter.26.cloned.1.call-done = bf16[256,6144]{0,1:T(8,128)(2,1)} async-done(((bf16[2048,6144]{0,1:T(8,128)(2,1)}), bf16[256,6144]{0,1:T(8,128)(2,1)}) %reduce-scatter.26.cloned.1.call-update) | async-done | bytes 3145744 | tf_op jit(solution)/shard_map/reduce_scatter | solution.py:179
  1289.9 101.7 %reduce-scatter.20.cloned.1.call-done = f32[64,512]{1,0:T(8,128)} async-done(((f32[2048,512]{1,0:T(8,128)}), f32[64,512]{1,0:T(8,128)}) %reduce-scatter.20.cloned.1.call-update) | async-done | bytes 131088 | tf_op jit(solution)/shard_map/reduce_scatter | solution.py:285
  1391.5 141.5 %reduce-scatter.22.cloned.1.call-done = f32[64,512]{1,0:T(8,128)} async-done(((f32[2048,512]{1,0:T(8,128)}), f32[64,512]{1,0:T(8,128)}) %reduce-scatter.22.cloned.1.call-update) | async-done | bytes 131088 | tf_op jit(solution)/shard_map/reduce_scatter | solution.py:286
  1533.1 216.4 %reduce-scatter.18.cloned.1.call-done = f32[64,2048]{1,0:T(8,128)} async-done(((f32[2048,2048]{1,0:T(8,128)}), f32[64,2048]{1,0:T(8,128)}) %reduce-scatter.18.cloned.1.call-update) | async-done | bytes 524304 | tf_op jit(solution)/shard_map/reduce_scatter | solution.py:284
  1749.5 187.4 %reduce-scatter.24.cloned.1.call-done = f32[64,2048]{1,0:T(8,128)} async-done(((f32[2048,2048]{1,0:T(8,128)}), f32[64,2048]{1,0:T(8,128)}) %reduce-scatter.24.cloned.1.call-update) | async-done | bytes 524304 | tf_op jit(solution)/shard_map/reduce_scatter | solution.py:287
  (145 shorter events, 125.7 us)
Async XLA Ops:
  7.2 60.6 %all-gather.12.cloned.1.call-start = ((), (), s32[]{:S(2)}) async-start(), calls=%async_computation.9 | async-start | bytes 2162688 | tf_op jit(solution)/shard_map/all_gather | solution.py:82
  7.9 117.8 %all-gather.14.cloned.1.call-start = ((), (), s32[]{:S(2)}) async-start(), calls=%async_computation.10 | async-start | bytes 2162688 | tf_op jit(solution)/shard_map/all_gather | solution.py:81
  8.7 196.9 %all-gather.16.cloned.1.call-start = ((), (), s32[]{:S(2)}) async-start(), calls=%async_computation.11 | async-start | bytes 8650752 | tf_op jit(solution)/shard_map/all_gather | solution.py:80
  9.4 274.6 %all-gather.18.cloned.1.call-start = ((), (), s32[]{:S(2)}) async-start(), calls=%async_computation.12 | async-start | bytes 8650752 | tf_op jit(solution)/shard_map/all_gather | solution.py:83
  10.0 395.4 %all-gather.20.cloned.1.call-start = ((), (), s32[]{:S(2)}) async-start(), calls=%async_computation.13 | async-start | bytes 9437184 | tf_op jit(solution)/shard_map/all_gather | solution.py:147
  10.6 421.2 %all-gather.28.cloned.1.call-start = ((), (), s32[]{:S(2)}) async-start(), calls=%async_computation.24 | async-start | bytes 2621440 | tf_op jit(solution)/shard_map/all_gather | solution.py:155
  62.5 66.1 %copy-start.1 = (bf16[1,128,2048]{2,1,0:T(8,128)(2,1)S(1)}, bf16[1,128,2048]{2,1,0:T(8,128)(2,1)}, u32[]{:S(2)}) copy-start(bf16[1,128,2048]{2,1,0:T(8,128)(2,1)} %param.13) | copy-start | bytes 1572868
  136.9 87.1 %copy-start.4 = (bf16[1,512,512]{1,2,0:T(8,128)(2,1)}, bf16[1,512,512]{1,2,0:T(8,128)(2,1)S(1)}, u32[]{:S(2)}) copy-start(bf16[1,512,512]{1,2,0:T(8,128)(2,1)S(1)} %all_gather.50) | copy-start | bytes 1572868
  223.9 5.4 copy-start.9
  226.0 5.4 copy-start.12
  289.7 265.0 %all-gather.22.cloned.1.call-start = ((), (), s32[]{:S(2)}) async-start(), calls=%async_computation.14 | async-start | bytes 9437184 | tf_op jit(solution)/shard_map/all_gather | solution.py:148
  290.5 290.3 %all-gather.26.cloned.1.call-start = ((), (), s32[]{:S(2)}) async-start(), calls=%async_computation.17 | async-start | bytes 2621440 | tf_op jit(solution)/shard_map/all_gather | solution.py:158
  291.2 412.9 %all-gather.24.cloned.1.call-start = ((), (), s32[]{:S(2)}) async-start(), calls=%async_computation.15 | async-start | bytes 9437184 | tf_op jit(solution)/shard_map/all_gather | solution.py:149
  292.0 476.2 %reduce-scatter.16.cloned.1.call-start = ((), (), s32[]{:S(2)}) async-start(), calls=%async_computation.18 | async-start | bytes 2621440 | tf_op jit(solution)/shard_map/reduce_scatter | solution.py:195
  716.2 8.0 copy-start.16
  716.2 8.0 copy-start.14
  731.6 66.4 %reduce-scatter.14.cloned.1.call-start = ((), (), s32[]{:S(2)}) async-start(), calls=%async_computation.16 | async-start | bytes 2621440 | tf_op jit(solution)/shard_map/reduce_scatter | solution.py:170
  731.7 19.5 %copy-start.13 = (f32[8,4,128]{2,1,0:T(4,128)S(1)}, f32[8,4,128]{2,1,0:T(4,128)}, u32[]{:S(2)}) copy-start(f32[8,4,128]{2,1,0:T(4,128)} %copy-done.12) | copy-start | bytes 49156
  741.6 122.1 %reduce-scatter.28.cloned.1.call-start = ((), (), s32[]{:S(2)}) async-start(), calls=%async_computation.25 | async-start | bytes 655360
  751.2 10.2 copy-start.15
  751.2 10.2 copy-start.17
  800.6 7.3 copy-start.10
  807.9 5.2 slice-start
  807.9 6.1 slice-start.1
  824.6 10.3 copy-start.11
  824.7 46.5 %reduce-scatter.30.cloned.1.call-start = ((), (), s32[]{:S(2)}) async-start(), calls=%async_computation.26 | async-start | bytes 655360
  844.5 433.7 %reduce-scatter.26.cloned.1.call-start = ((), (), s32[]{:S(2)}) async-start(), calls=%async_computation.23 | async-start | bytes 28311552 | tf_op jit(solution)/shard_map/reduce_scatter | solution.py:179
  863.6 528.0 %reduce-scatter.20.cloned.1.call-start = ((), (), s32[]{:S(2)}) async-start(), calls=%async_computation.20 | async-start | bytes 4325376 | tf_op jit(solution)/shard_map/reduce_scatter | solution.py:285
  867.8 665.3 %reduce-scatter.22.cloned.1.call-start = ((), (), s32[]{:S(2)}) async-start(), calls=%async_computation.21 | async-start | bytes 4325376 | tf_op jit(solution)/shard_map/reduce_scatter | solution.py:286
  875.3 874.2 %reduce-scatter.18.cloned.1.call-start = ((), (), s32[]{:S(2)}) async-start(), calls=%async_computation.19 | async-start | bytes 17301504 | tf_op jit(solution)/shard_map/reduce_scatter | solution.py:284
  887.9 1048.9 %reduce-scatter.24.cloned.1.call-start = ((), (), s32[]{:S(2)}) async-start(), calls=%async_computation.22 | async-start | bytes 17301504 | tf_op jit(solution)/shard_map/reduce_scatter | solution.py:287
  896.1 6.5 copy-start.3
  (6 other events, 17.3 us)
Sparse Core Ops, SparseCore 0:
  10.8 56.9 all-gather.11
  70.7 55.0 all-gather.13
  128.6 76.8 all-gather.15
  208.3 75.6 all-gather.17
  285.9 119.3 all-gather.19
  407.3 24.4 all-gather.27
  433.9 120.7 all-gather.21
  556.3 24.4 all-gather.25
  582.8 121.2 all-gather.23
  731.7 32.4 reduce-scatter.15
  766.8 31.1 reduce-scatter.13
  824.8 21.6 reduce-scatter.27
  849.5 21.6 reduce-scatter.29
  874.9 403.1 reduce-scatter.25
  1280.9 110.6 reduce-scatter.19
  1394.3 138.7 reduce-scatter.21
  1535.8 213.6 reduce-scatter.17
  1752.2 184.5 reduce-scatter.23
where the time goes:
time: 1950 us; the launch traced here: 1940 us
  waiting for transfers between devices  1580 us (81%)
  matrix products  157 us (8%)
  blocking collectives  104 us (5%)
  local copies, waits for them, and re-layouts  45.6 us (2%)
  other arithmetic  34.6 us (2%)
    reduce_scatter x1, waiting for transfers between devices, body(): lax.psum_scatter(jnp.concatenate([tdot(h_group, d_gate), tdot(h_group, d_...  329 us
    reduce_scatter x1, waiting for transfers between devices, body(): lax.psum_scatter(query_term, ('dp', 'ctx'), scatter_dimension=0, tiled=True)  216 us
    reduce_scatter x1, waiting for transfers between devices, body(): lax.psum_scatter(out_term, ('dp', 'ctx'), scatter_dimension=0, tiled=True)  187 us
    reduce_scatter x1, waiting for transfers between devices, body(): lax.psum_scatter(value_term, ('dp', 'ctx'), scatter_dimension=0, tiled=True)  142 us
    all_gather x1, waiting for transfers between devices, body(): lax.all_gather(w_down, 'dp', axis=1, tiled=True)  123 us
    all_gather x1, waiting for transfers between devices, body(): lax.all_gather(w_gate, 'dp', axis=0, tiled=True)  113 us
    all_gather x1, waiting for transfers between devices, body(): lax.all_gather(w_up, 'dp', axis=0, tiled=True)  112 us
    reduce_scatter x1, waiting for transfers between devices, body(): lax.psum_scatter(key_term, ('dp', 'ctx'), scatter_dimension=0, tiled=True)  102 us
  transfers between devices with their start and end apart: 18, of which 16 were waited for; matrix products, arithmetic and copies ran while one was open for 9% of the time, Pallas kernels for 0%

commit v1 on v0

--- a/solution.py
+++ b/solution.py
@@ -9,6 +9,23 @@
 EPS_NORM = 1e-05
 ROPE_BASE = 500000.0
 MASKED = -1e30
+
+
+def laid_out(blocks, dim):
+    blocks = jnp.moveaxis(blocks, 0, dim)
+    shape = blocks.shape
+    return blocks.reshape(*shape[:dim], shape[dim] * shape[dim + 1], *shape[dim + 2 :])
+
+
+def gather_around(x, axis, dim):
+    size = lax.axis_size(axis)
+    forward = [(i, (i + 1) % size) for i in range(size)]
+    pieces = [x]
+    while len(pieces) < size:
+        pieces.append(lax.ppermute(pieces[-1], axis, forward))
+    here = lax.axis_index(axis)
+    pieces = jnp.stack(pieces)[(here - jnp.arange(size)) % size]
+    return laid_out(pieces, dim)
 
 
 def rope_tables(where_pos, half_width):
@@ -145,7 +162,7 @@
     resid = xfloat + jnp.dot(attended, output_weight, preferred_element_type=jnp.float32)
     wgate, wup_proj, wdown = (
         lax.all_gather(w_gate, "dp", axis=0, tiled=True),
-        lax.all_gather(w_up, "dp", axis=0, tiled=True),
+        gather_around(w_up, "dp", 0),
         lax.all_gather(w_down, "dp", axis=1, tiled=True),
     )
     inv_two = lax.rsqrt(jnp.mean(resid * resid, axis=-1, keepdims=True) + EPS_NORM)

time: 1950 us -> 1880 us (0.964)
  waiting for transfers between devices: 1580 us -> 1470 us
  local copies, waits for them, and re-layouts: 45.6 us -> 66.8 us
    all_gather x1 -> x0, waiting for transfers between devices: 112 us -> none  [body(): lax.all_gather(w_up, 'dp', axis=0, tiled=True)]
    ppermute x0 -> x7, waiting for transfers between devices: none -> 82.4 us  [gather_around(): pieces.append(lax.ppermute(pieces[-1], axis, forward))]
    all_gather x1, waiting for transfers between devices: 47.4 us -> 0.01 us  [body(): lax.all_gather(w_key, ('dp', 'ctx'), axis=0, tiled=True)]
    reduce_scatter x1, waiting for transfers between devices: 142 us -> 101 us  [body(): lax.psum_scatter(value_term, ('dp', 'ctx'), scatter_dimension=0, tiled=True)]
    reduce_scatter x1, waiting for transfers between devices: 102 us -> 141 us  [body(): lax.psum_scatter(key_term, ('dp', 'ctx'), scatter_dimension=0, tiled=True)]
    reduce_scatter x1, waiting for transfers between devices: 187 us -> 217 us  [body(): lax.psum_scatter(out_term, ('dp', 'ctx'), scatter_dimension=0, tiled=True)]
    reduce_scatter x1, waiting for transfers between devices: 216 us -> 187 us  [body(): lax.psum_scatter(query_term, ('dp', 'ctx'), scatter_dimension=0, tiled=True)]
  transfers between devices with their start and end apart: 18 -> 24, of which waited for: 16 -> 17; matrix products, arithmetic and copies ran while one was open for 9% -> 10% of each run, Pallas kernels for 0% -> 0%
where the time goes in v1:
time: 1880 us
  waiting for transfers between devices  1470 us (78%)
  matrix products  149 us (8%)
  blocking collectives  122 us (6%)
  local copies, waits for them, and re-layouts  66.8 us (4%)
  other arithmetic  37.5 us (2%)
    reduce_scatter x1, waiting for transfers between devices, body(): lax.psum_scatter(jnp.concatenate([tdot(h_group, d_gate), tdot(h_group, d_...  329 us
    reduce_scatter x1, waiting for transfers between devices, body(): lax.psum_scatter(out_term, ('dp', 'ctx'), scatter_dimension=0, tiled=True)  217 us
    reduce_scatter x1, waiting for transfers between devices, body(): lax.psum_scatter(query_term, ('dp', 'ctx'), scatter_dimension=0, tiled=True)  187 us
    reduce_scatter x1, waiting for transfers between devices, body(): lax.psum_scatter(key_term, ('dp', 'ctx'), scatter_dimension=0, tiled=True)  141 us
    all_gather x1, waiting for transfers between devices, body(): lax.all_gather(w_gate, 'dp', axis=0, tiled=True)  114 us
    all_gather x1, waiting for transfers between devices, body(): lax.all_gather(w_down, 'dp', axis=1, tiled=True)  105 us
    reduce_scatter x1, waiting for transfers between devices, body(): lax.psum_scatter(value_term, ('dp', 'ctx'), scatter_dimension=0, tiled=True)  101 us
    unnamed x2, blocking collectives  99.2 us
  transfers between devices with their start and end apart: 24, of which 17 were waited for; matrix products, arithmetic and copies ran while one was open for 10% of the time, Pallas kernels for 0%

profile of v1, /device:TPU:13, one launch (start us, length us, event | category | flops | bytes accessed | tf_op | source)
XLA Modules:
  0.0 1877.1 jit_solution(15910090893129224082)
XLA Ops:
  13.2 23.5 %collective-permute-done = bf16[256,2048]{1,0:T(8,128)(2,1)S(1)} collective-permute-done((bf16[256,2048]{1,0:T(8,128)(2,1)}, bf16[256,2048]{1,0:T(8,128)(2,1)S(1)}, u32[]{:S(2)}, u32[]{:S(2)}) %collective-permute-start) | collective-permute-done | bytes 1048608 | tf_op jit(solution)/shard_map/ppermute | solution.py:25
  48.5 15.0 collective-permute-done.1
  70.0 22.9 %collective-permute-done.2 = bf16[256,2048]{1,0:T(8,128)(2,1)S(1)} collective-permute-done((bf16[256,2048]{1,0:T(8,128)(2,1)}, bf16[256,2048]{1,0:T(8,128)(2,1)S(1)}, u32[]{:S(2)}, u32[]{:S(2)}) %collective-permute-start.2) | collective-permute-done | bytes 1048608 | tf_op jit(solution)/shard_map/ppermute | solution.py:25
  97.7 57.3 %all-reduce.5 = (bf16[2048]{0:T(1024)(128)(2,1)S(1)}, bf16[2048]{0:T(1024)(128)(2,1)S(1)}) all-reduce(bf16[2048]{0:T(1024)(128)(2,1)S(1)} %dynamic-update-slice, bf16[2048]{0:T(1024)(128)(2,1)S(1)} %dynamic-update-slice.1), channel_id=1, replica_groups=mesh['dp'=8,'ctx'=4] {'dp','ctx'}, use_global_device_ids=true, to_apply=%add | all-reduce | flops 4096 | bytes 16384
  163.0 8.6 all-gather
  191.6 65.1 %all-gather.15.cloned.1.call-done = bf16[2048,2048]{1,0:T(8,128)(2,1)} async-done(((bf16[64,2048]{1,0:T(8,128)(2,1)}), bf16[2048,2048]{1,0:T(8,128)(2,1)}) %all-gather.15.cloned.1.call-update) | async-done | bytes 8388624 | tf_op jit(solution)/shard_map/all_gather | solution.py:97
  256.7 12.4 copy.48
  282.8 55.2 %all-gather.17.cloned.1.call-done = bf16[2048,2048]{1,0:T(8,128)(2,1)} async-done(((bf16[64,2048]{1,0:T(8,128)(2,1)}), bf16[2048,2048]{1,0:T(8,128)(2,1)}) %all-gather.17.cloned.1.call-update) | async-done | bytes 8388624 | tf_op jit(solution)/shard_map/all_gather | solution.py:100
  354.1 17.0 collective-permute-done.6
  372.1 8.3 gather_fusion
  380.5 104.5 %all-gather.21.cloned.1.call-done = bf16[2048,2048]{1,0:T(8,128)(2,1)} async-done(((bf16[2048,256]{1,0:T(8,128)(2,1)}), bf16[2048,2048]{1,0:T(8,128)(2,1)}) %all-gather.21.cloned.1.call-update) | async-done | bytes 8388624 | tf_op jit(solution)/shard_map/all_gather | solution.py:166
  485.0 10.6 fusion.13
  495.6 114.3 %all-gather.19.cloned.1.call-done = bf16[2048,2048]{1,0:T(8,128)(2,1)} async-done(((bf16[256,2048]{1,0:T(8,128)(2,1)}), bf16[2048,2048]{1,0:T(8,128)(2,1)}) %all-gather.19.cloned.1.call-update) | async-done | bytes 8388624 | tf_op jit(solution)/shard_map/all_gather | solution.py:164
  609.8 26.6 %all-gather.25.cloned.1.call-done = bf16[512,2048]{1,0:T(8,128)(2,1)} async-done(((bf16[128,2048]{1,0:T(8,128)(2,1)}), bf16[512,2048]{1,0:T(8,128)(2,1)}) %all-gather.25.cloned.1.call-update) | async-done | bytes 2097168 | tf_op jit(solution)/shard_map/all_gather | solution.py:172
  636.4 7.7 fusion.82
  644.1 11.3 multiply_convert_fusion
  655.4 7.9 fusion.83
  663.4 7.8 fusion.11
  671.3 9.9 fusion.10
  681.2 10.2 convolution_convert_fusion
  706.8 28.7 %reduce-scatter.14.cloned.1.call-done = bf16[1,128,2048]{2,1,0:T(8,128)(2,1)} async-done(((bf16[1,512,2048]{2,1,0:T(8,128)(2,1)}), bf16[1,128,2048]{2,1,0:T(8,128)(2,1)}) %reduce-scatter.14.cloned.1.call-update) | async-done | bytes 524304 | tf_op jit(solution)/shard_map/reduce_scatter | solution.py:187
  758.1 7.6 fusion.4
  771.1 18.0 pad_maximum_fusion
  793.4 11.1 reduce-scatter.28.cloned.1.call-done
  808.7 9.0 fusion.61
  822.0 8.2 fusion.52
  838.6 41.9 %all-reduce.4 = (f32[2048]{0:T(1024)S(1)}, f32[2048]{0:T(1024)S(1)}) all-reduce(f32[2048]{0:T(1024)S(1)} %get-tuple-element.46, f32[2048]{0:T(1024)S(1)} %get-tuple-element.44), channel_id=8, replica_groups=mesh['dp'=8,'ctx'=4] {'dp','ctx'}, use_global_device_ids=true, to_apply=%region_11.12.clone | all-reduce | flops 4096 | bytes 32768
  883.0 328.6 %reduce-scatter.26.cloned.1.call-done = bf16[256,6144]{0,1:T(8,128)(2,1)} async-done(((bf16[2048,6144]{0,1:T(8,128)(2,1)}), bf16[256,6144]{0,1:T(8,128)(2,1)}) %reduce-scatter.26.cloned.1.call-update) | async-done | bytes 3145744 | tf_op jit(solution)/shard_map/reduce_scatter | solution.py:196
  1223.3 101.4 %reduce-scatter.22.cloned.1.call-done = f32[64,512]{1,0:T(8,128)} async-done(((f32[2048,512]{1,0:T(8,128)}), f32[64,512]{1,0:T(8,128)}) %reduce-scatter.22.cloned.1.call-update) | async-done | bytes 131088 | tf_op jit(solution)/shard_map/reduce_scatter | solution.py:303
  1324.8 141.4 %reduce-scatter.20.cloned.1.call-done = f32[64,512]{1,0:T(8,128)} async-done(((f32[2048,512]{1,0:T(8,128)}), f32[64,512]{1,0:T(8,128)}) %reduce-scatter.20.cloned.1.call-update) | async-done | bytes 131088 | tf_op jit(solution)/shard_map/reduce_scatter | solution.py:302
  1466.2 216.7 %reduce-scatter.24.cloned.1.call-done = f32[64,2048]{1,0:T(8,128)} async-done(((f32[2048,2048]{1,0:T(8,128)}), f32[64,2048]{1,0:T(8,128)}) %reduce-scatter.24.cloned.1.call-update) | async-done | bytes 524304 | tf_op jit(solution)/shard_map/reduce_scatter | solution.py:304
  1682.9 187.4 %reduce-scatter.18.cloned.1.call-done = f32[64,2048]{1,0:T(8,128)} async-done(((f32[2048,2048]{1,0:T(8,128)}), f32[64,2048]{1,0:T(8,128)}) %reduce-scatter.18.cloned.1.call-update) | async-done | bytes 524304 | tf_op jit(solution)/shard_map/reduce_scatter | solution.py:301
  (198 shorter events, 166.1 us)
Async XLA Ops:
  7.2 153.7 %copy-start.1 = (bf16[1,128,2048]{2,1,0:T(8,128)(2,1)S(1)}, bf16[1,128,2048]{2,1,0:T(8,128)(2,1)}, u32[]{:S(2)}) copy-start(bf16[1,128,2048]{2,1,0:T(8,128)(2,1)} %param.13) | copy-start | bytes 1572868
  7.2 153.7 %all-gather.11.cloned.1.call-start = ((), (), s32[]{:S(2)}) async-start(), calls=%async_computation.9 | async-start | bytes 2162688 | tf_op jit(solution)/shard_map/all_gather | solution.py:99
  7.9 164.7 %all-gather.13.cloned.1.call-start = ((), (), s32[]{:S(2)}) async-start(), calls=%async_computation.10 | async-start | bytes 2162688 | tf_op jit(solution)/shard_map/all_gather | solution.py:98
  8.7 248.1 %all-gather.15.cloned.1.call-start = ((), (), s32[]{:S(2)}) async-start(), calls=%async_computation.11 | async-start | bytes 8650752 | tf_op jit(solution)/shard_map/all_gather | solution.py:97
  9.4 328.6 %all-gather.17.cloned.1.call-start = ((), (), s32[]{:S(2)}) async-start(), calls=%async_computation.12 | async-start | bytes 8650752 | tf_op jit(solution)/shard_map/all_gather | solution.py:100
  10.0 370.5 %all-gather.23.cloned.1.call-start = ((), (), s32[]{:S(2)}) async-start(), calls=%async_computation.16 | async-start | bytes 2621440 | tf_op jit(solution)/shard_map/all_gather | solution.py:175
  10.6 474.4 %all-gather.21.cloned.1.call-start = ((), (), s32[]{:S(2)}) async-start(), calls=%async_computation.14 | async-start | bytes 9437184 | tf_op jit(solution)/shard_map/all_gather | solution.py:166
  11.1 598.7 %all-gather.19.cloned.1.call-start = ((), (), s32[]{:S(2)}) async-start(), calls=%async_computation.13 | async-start | bytes 9437184 | tf_op jit(solution)/shard_map/all_gather | solution.py:164
  11.9 624.5 %all-gather.25.cloned.1.call-start = ((), (), s32[]{:S(2)}) async-start(), calls=%async_computation.23 | async-start | bytes 2621440 | tf_op jit(solution)/shard_map/all_gather | solution.py:172
  11.9 24.8 %collective-permute-start = (bf16[256,2048]{1,0:T(8,128)(2,1)}, bf16[256,2048]{1,0:T(8,128)(2,1)S(1)}, u32[]{:S(2)}, u32[]{:S(2)}) collective-permute-start(bf16[256,2048]{1,0:T(8,128)(2,1)} %param.23), channel_id=1, source_target_pairs={{0,4},{4,8},{8,12},{12,16},{16,20},{20,24},{24,28},{28,0},{1,5},{5... | collective-permute-start | bytes 3145736 | tf_op jit(solution)/shard_map/ppermute | solution.py:25
  36.8 26.7 %collective-permute-start.1 = (bf16[256,2048]{1,0:T(8,128)(2,1)S(1)}, bf16[256,2048]{1,0:T(8,128)(2,1)}, u32[]{:S(2)}, u32[]{:S(2)}) collective-permute-start(bf16[256,2048]{1,0:T(8,128)(2,1)S(1)} %collective-permute-done), channel_id=1, source_target_pairs={{0,4},{4,8},{8,12},{12,16},{16,20},{20,24},{24,28},{28,0},{1,5},{5... | collective-permute-start | bytes 3145736 | tf_op jit(solution)/shard_map/ppermute | solution.py:25
  48.5 220.6 %copy-start.22 = (f32[128]{0:T(128)}, f32[128]{0:T(128)S(1)}, u32[]{:S(2)}) copy-start(f32[128]{0:T(128)S(1)} %add_rsqrt_fusion.1) | copy-start | bytes 1540
  63.5 29.4 %collective-permute-start.2 = (bf16[256,2048]{1,0:T(8,128)(2,1)}, bf16[256,2048]{1,0:T(8,128)(2,1)S(1)}, u32[]{:S(2)}, u32[]{:S(2)}) collective-permute-start(bf16[256,2048]{1,0:T(8,128)(2,1)} %collective-permute-done.1), channel_id=1, source_target_pairs={{0,4},{4,8},{8,12},{12,16},{16,20},{20,24},{24,28},{28,0},{1,5},{5... | collective-permute-start | bytes 3145736 | tf_op jit(solution)/shard_map/ppermute | solution.py:25
  66.9 208.2 %copy-start.18 = (f32[128,32]{0,1:T(8,128)}, f32[128,32]{0,1:T(8,128)S(1)}, u32[]{:S(2)}) copy-start(f32[128,32]{0,1:T(8,128)S(1)} %get-tuple-element.67) | copy-start | bytes 49156
  66.9 208.2 %copy-start.20 = (f32[128,32]{0,1:T(8,128)}, f32[128,32]{0,1:T(8,128)S(1)}, u32[]{:S(2)}) copy-start(f32[128,32]{0,1:T(8,128)S(1)} %get-tuple-element.68) | copy-start | bytes 49156
  93.0 67.9 %copy-start.12 = (bf16[256,2048]{1,0:T(8,128)(2,1)}, bf16[256,2048]{1,0:T(8,128)(2,1)S(1)}, u32[]{:S(2)}) copy-start(bf16[256,2048]{1,0:T(8,128)(2,1)S(1)} %collective-permute-done.2) | copy-start | bytes 3145732
  93.0 65.4 %collective-permute-start.3 = (bf16[256,2048]{1,0:T(8,128)(2,1)S(1)}, bf16[256,2048]{1,0:T(8,128)(2,1)}, u32[]{:S(2)}, u32[]{:S(2)}) collective-permute-start(bf16[256,2048]{1,0:T(8,128)(2,1)S(1)} %collective-permute-done.2), channel_id=1, source_target_pairs={{0,4},{4,8},{8,12},{12,16},{16,20},{20,24},{24,28},{28,0},{1,5},{5... | collective-permute-start | bytes 3145736 | tf_op jit(solution)/shard_map/ppermute | solution.py:25
  155.0 114.1 %copy-start.13 = (f32[2048]{0:T(1024)}, f32[2048]{0:T(1024)S(1)}, u32[]{:S(2)}) copy-start(f32[2048]{0:T(1024)S(1)} %convert_element_type.206) | copy-start | bytes 24580
  158.4 29.6 %collective-permute-start.4 = (bf16[256,2048]{1,0:T(8,128)(2,1)}, bf16[256,2048]{1,0:T(8,128)(2,1)}, u32[]{:S(2)}, u32[]{:S(2)}) collective-permute-start(bf16[256,2048]{1,0:T(8,128)(2,1)} %collective-permute-done.3), channel_id=1, source_target_pairs={{0,4},{4,8},{8,12},{12,16},{16,20},{20,24},{24,28},{28,0},{1,5},{5... | collective-permute-start | bytes 3145736 | tf_op jit(solution)/shard_map/ppermute | solution.py:25
  184.1 91.2 %copy-start.6 = (bf16[1,512,512]{1,2,0:T(8,128)(2,1)}, bf16[1,512,512]{1,2,0:T(8,128)(2,1)S(1)}, u32[]{:S(2)}) copy-start(bf16[1,512,512]{1,2,0:T(8,128)(2,1)S(1)} %all_gather.47) | copy-start | bytes 1572868
  187.9 158.3 %collective-permute-start.5 = (bf16[256,2048]{1,0:T(8,128)(2,1)}, bf16[256,2048]{1,0:T(8,128)(2,1)}, u32[]{:S(2)}, u32[]{:S(2)}) collective-permute-start(bf16[256,2048]{1,0:T(8,128)(2,1)} %collective-permute-done.4), channel_id=1, source_target_pairs={{0,4},{4,8},{8,12},{12,16},{16,20},{20,24},{24,28},{28,0},{1,5},{5... | collective-permute-start | bytes 3145736 | tf_op jit(solution)/shard_map/ppermute | solution.py:25
  282.8 60.0 %copy-start.4 = (bf16[8,64,4,128]{3,1,2,0:T(8,128)(2,1)}, bf16[8,64,4,128]{3,1,2,0:T(8,128)(2,1)S(1)}, u32[]{:S(2)}) copy-start(bf16[8,64,4,128]{3,1,2,0:T(8,128)(2,1)S(1)} %fusion.24) | copy-start | bytes 1572868
  343.8 361.6 %reduce-scatter.16.cloned.1.call-start = ((), (), s32[]{:S(2)}) async-start(), calls=%async_computation.17 | async-start | bytes 2621440 | tf_op jit(solution)/shard_map/reduce_scatter | solution.py:212
  346.2 24.9 %collective-permute-start.6 = (bf16[256,2048]{1,0:T(8,128)(2,1)}, bf16[256,2048]{1,0:T(8,128)(2,1)S(1)}, u32[]{:S(2)}, u32[]{:S(2)}) collective-permute-start(bf16[256,2048]{1,0:T(8,128)(2,1)} %collective-permute-done.5), channel_id=1, source_target_pairs={{0,4},{4,8},{8,12},{12,16},{16,20},{20,24},{24,28},{28,0},{1,5},{5... | collective-permute-start | bytes 3145736 | tf_op jit(solution)/shard_map/ppermute | solution.py:25
  671.2 64.4 %reduce-scatter.14.cloned.1.call-start = ((), (), s32[]{:S(2)}) async-start(), calls=%async_computation.15 | async-start | bytes 2621440 | tf_op jit(solution)/shard_map/reduce_scatter | solution.py:187
  681.1 108.1 %reduce-scatter.30.cloned.1.call-start = ((), (), s32[]{:S(2)}) async-start(), calls=%async_computation.25 | async-start | bytes 655360
  758.1 46.4 %reduce-scatter.28.cloned.1.call-start = ((), (), s32[]{:S(2)}) async-start(), calls=%async_computation.24 | async-start | bytes 655360
  771.1 440.6 %reduce-scatter.26.cloned.1.call-start = ((), (), s32[]{:S(2)}) async-start(), calls=%async_computation.22 | async-start | bytes 28311552 | tf_op jit(solution)/shard_map/reduce_scatter | solution.py:196
  789.2 535.6 %reduce-scatter.22.cloned.1.call-start = ((), (), s32[]{:S(2)}) async-start(), calls=%async_computation.20 | async-start | bytes 4325376 | tf_op jit(solution)/shard_map/reduce_scatter | solution.py:303
  793.4 672.9 %reduce-scatter.20.cloned.1.call-start = ((), (), s32[]{:S(2)}) async-start(), calls=%async_computation.19 | async-start | bytes 4325376 | tf_op jit(solution)/shard_map/reduce_scatter | solution.py:302
  808.7 874.3 %reduce-scatter.24.cloned.1.call-start = ((), (), s32[]{:S(2)}) async-start(), calls=%async_computation.21 | async-start | bytes 17301504 | tf_op jit(solution)/shard_map/reduce_scatter | solution.py:304
  817.7 1052.6 %reduce-scatter.18.cloned.1.call-start = ((), (), s32[]{:S(2)}) async-start(), calls=%async_computation.18 | async-start | bytes 17301504 | tf_op jit(solution)/shard_map/reduce_scatter | solution.py:301
  (27 other events, 260.1 us)
Sparse Core Ops, SparseCore 0:
  10.9 81.6 all-gather.10
  95.4 68.9 all-gather.12
  167.3 89.4 all-gather.14
  259.5 78.5 all-gather.16
  339.4 21.1 all-gather.22
  362.5 122.4 all-gather.20
  487.1 122.6 all-gather.18
  611.9 24.4 all-gather.24
  671.3 30.6 reduce-scatter.15
  704.3 31.1 reduce-scatter.13
  758.2 21.6 reduce-scatter.29
  782.8 21.6 reduce-scatter.27
  808.4 403.1 reduce-scatter.25
  1214.3 110.4 reduce-scatter.21
  1327.5 138.6 reduce-scatter.19
  1468.9 213.9 reduce-scatter.23
  1685.7 184.6 reduce-scatter.17
